TPU v7x, 32 devices: a whole 2x2x4 slice. The times are simulated.
32 devices in a mesh: gx: 8 (over z, x), gy: 4 (over y, core).
Axes of the slice: x: 2, y: 2, z: 4, core: 2. Of those that a mesh axis runs over, the one named last changes fastest.
Arguments:
- right_side: float32 [32, 256, 2048], P(None, 'gx', 'gy'), may hold values from -6 to 6
- absorb: float32 [256, 2048], P('gx', 'gy'), may hold values from 0.05 to 4
- tiles: float32 [2, 1024, 512], replicated, may hold values from -0.0078125 to 0.0078125
- tile_index: int32 [256, 4], P('gx', 'gy'), may hold values from 0 to 1
- tile_sign: int32 [256, 4], P('gx', 'gy'), may hold values from 0 to 1
Outputs:
- solution: float32 [32, 256, 2048], P(None, 'gx', 'gy')
- residual: float32 [32, 256, 2048], P(None, 'gx', 'gy')
- sketched_residual: float32 [32, 1024], P(None, ('gx', 'gy'))
Inputs may be any that keep to these rules, and one draw needn't show every extreme that they name: `tile_index`: which of the 2 tiles a row of a column block uses. `tile_sign`: 1 stands for the sign +1, 0 for -1.
All inputs are finite; a program needn't handle non-finite values.
Results may differ from a plain program's by a relative error of at most 0.006.
Values sent between devices are 32-bit elements; how exact they have to be, the bound alone decides.
A program may use at most 64 MiB of HBM per device.

v0:
```python
import jax
import jax.numpy as jnp
from jax import lax
from jax.sharding import PartitionSpec as P

axial_x = 1.0
axial_y = 0.2
shear_half = 0.15
ridge_share = 1e-05


def padded_2(cells, sides, width):
    for axis, dim in sides:
        count = lax.axis_size(axis)
        ends = count - 1
        head = lax.slice_in_dim(cells, 0, width, axis=dim)
        tail = lax.slice_in_dim(cells, cells.shape[dim] - width, cells.shape[dim], axis=dim)
        cells = jnp.concatenate(
            [
                lax.ppermute(tail, axis, [(i, (i + 1) % count) for i in range(ends)]),
                cells,
                lax.ppermute(head, axis, [((i + 1) % count, i) for i in range(ends)]),
            ],
            axis=dim,
        )
    return cells


def operate(padded, absorb):
    center = padded[..., 1:-1, 1:-1]
    east_side = padded[..., 1:-1, 2:]
    west_side = padded[..., 1:-1, :-2]
    north_side = padded[..., :-2, 1:-1]
    south_side = padded[..., 2:, 1:-1]
    upper_right = padded[..., :-2, 2:]
    upper_left = padded[..., :-2, :-2]
    lower_right = padded[..., 2:, 2:]
    lower_left = padded[..., 2:, :-2]
    diagonal_weight = 2.0 * axial_x + 2.0 * axial_y
    lapl = (
        diagonal_weight * center
        - axial_x * (east_side + west_side)
        - axial_y * (north_side + south_side)
    )
    lapl = lapl - shear_half * (upper_right + lower_left) + shear_half * (upper_left + lower_right)
    return (lapl + absorb * center) / (diagonal_weight + absorb)


def sketch_field(field, tiles, tile_index, tile_sign):
    blocks = field.reshape(field.shape[0], tile_index.shape[0], tile_index.shape[1], tiles.shape[2])
    which = jnp.arange(tiles.shape[0], dtype=jnp.int32)
    signed = (2 * tile_sign - 1).astype(jnp.float32)
    picker = (tile_index[..., None] == which).astype(jnp.float32) * signed[..., None]
    folded = jnp.einsum("rgk,qrgc->qkc", picker, blocks, precision=lax.Precision.HIGHEST)
    return jnp.einsum("ksc,qkc->qs", tiles, folded, precision=lax.Precision.HIGHEST)


def local_products(sketches):
    basis_sketch = sketches[1:]
    gram_matrix = jnp.einsum(
        "iqs,jqs->ijq", basis_sketch, basis_sketch, precision=lax.Precision.HIGHEST
    )
    projected = jnp.einsum("iqs,qs->iq", basis_sketch, sketches[0], precision=lax.Precision.HIGHEST)
    return (gram_matrix, projected)


def coefficients(gram_matrix, projected):
    ridge_term = ridge_share * (gram_matrix[0, 0] + gram_matrix[1, 1] + gram_matrix[2, 2])
    first_pivot = jnp.sqrt(gram_matrix[0, 0] + ridge_term)
    lower_10 = gram_matrix[1, 0] / first_pivot
    lower_20 = gram_matrix[2, 0] / first_pivot
    second_pivot = jnp.sqrt(gram_matrix[1, 1] + ridge_term - lower_10 * lower_10)
    lower_21 = (gram_matrix[2, 1] - lower_20 * lower_10) / second_pivot
    third_pivot = jnp.sqrt(
        gram_matrix[2, 2] + ridge_term - lower_20 * lower_20 - lower_21 * lower_21
    )
    forward_0 = projected[0] / first_pivot
    forward_1 = (projected[1] - lower_10 * forward_0) / second_pivot
    forward_2 = (projected[2] - lower_20 * forward_0 - lower_21 * forward_1) / third_pivot
    coeff_2 = forward_2 / third_pivot
    coeff_1 = (forward_1 - lower_21 * coeff_2) / second_pivot
    coeff_0 = (forward_0 - lower_10 * coeff_1 - lower_20 * coeff_2) / first_pivot
    return jnp.stack([coeff_0, coeff_1, coeff_2])


def reduce_one(partial_sketch):
    return lax.psum(partial_sketch, ("gx", "gy"))


def own_rows(full_sketch):
    devices = lax.axis_size("gx") * lax.axis_size("gy")
    width = full_sketch.shape[-1] // devices
    start = lax.axis_index(("gx", "gy")) * width
    return lax.dynamic_slice_in_dim(full_sketch, start, width, full_sketch.ndim - 1)


def shards(right_side, absorb, tiles, tile_index, tile_sign):
    count_rhs = right_side.shape[0]
    row_count = right_side.shape[1]
    col_count = right_side.shape[2]
    basis = [right_side]
    stacked = jnp.concatenate([right_side, absorb[None]], 0)
    widened = padded_2(stacked, (("gx", 1), ("gy", 2)), 3)
    current = widened[:count_rhs]
    absorb_wide = widened[count_rhs]
    row_global = lax.axis_index("gx") * row_count + jnp.arange(row_count + 6, dtype=jnp.int32) - 3
    col_global = lax.axis_index("gy") * col_count + jnp.arange(col_count + 6, dtype=jnp.int32) - 3
    row_inside = (row_global >= 0) & (row_global < row_count * lax.axis_size("gx"))
    col_inside = (col_global >= 0) & (col_global < col_count * lax.axis_size("gy"))
    inside_grid = (row_inside[:, None] & col_inside[None, :]).astype(jnp.float32)
    for step in range(1, 4):
        stop_row = row_count + 6 - step
        stop_col = col_count + 6 - step
        current = (
            operate(current, absorb_wide[step:stop_row, step:stop_col])
            * inside_grid[step:stop_row, step:stop_col]
        )
        margin = 3 - step
        basis.append(current[:, margin : margin + row_count, margin : margin + col_count])
    partials = [sketch_field(field, tiles, tile_index, tile_sign) for field in basis]
    sketches = jnp.stack([reduce_one(partial_sketch) for partial_sketch in partials])
    gram_matrix, projected = local_products(sketches)
    coeff = coefficients(gram_matrix, projected)
    full_residual = sketches[0] - jnp.einsum(
        "jq,jqs->qs", coeff, sketches[1:], precision=lax.Precision.HIGHEST
    )
    sketched_residual = own_rows(full_residual)
    solution = (
        coeff[0][:, None, None] * basis[0]
        + coeff[1][:, None, None] * basis[1]
        + coeff[2][:, None, None] * basis[2]
    )
    residual = right_side - (
        coeff[0][:, None, None] * basis[1]
        + coeff[1][:, None, None] * basis[2]
        + coeff[2][:, None, None] * basis[3]
    )
    return (solution, residual, sketched_residual)


def solution(mesh):
    in_specs = (P(None, "gx", "gy"), P("gx", "gy"), P(), P("gx", "gy"), P("gx", "gy"))
    out_specs = (P(None, "gx", "gy"), P(None, "gx", "gy"), P(None, ("gx", "gy")))
    return jax.shard_map(shards, mesh=mesh, in_specs=in_specs, out_specs=out_specs, check_vma=False)
```

profile of v0, /device:TPU:0, one launch (start us, length us, event | category | flops | bytes accessed | tf_op | source)
XLA Modules:
  0.0 244.2 jit_solution(11571868606420895437)
XLA Ops:
  7.2 1.5 pad_maximum_fusion.7
  8.8 4.9 %collective-permute-start = (f32[33,3,512]{2,0,1:T(8,128)S(1)}, f32[33,3,512]{2,0,1:T(8,128)S(1)}, u32[]{:S(2)}, u32[]{:S(2)}) collective-permute-start(f32[33,3,512]{2,0,1:T(8,128)S(1)} %copy.13), channel_id=1, source_target_pairs={{0,4},{4,8},{8,12},{12,16},{16,20},{20,24},{24,28},{1,5},{5,9},{9,... | collective-permute-start | bytes 608264 | tf_op jit(solution)/shard_map/ppermute | solution.py:20
  13.8 1.3 collective-permute-start.1
  15.7 1.1 convolution_bitcast_fusion.5
  16.8 6.7 %convolution_bitcast_fusion.3 = f32[32,1024]{1,0:T(8,128)} fusion(f32[2,1024,512]{2,1,0:T(8,128)} %param.7, f32[32,2,512]{2,1,0:T(2,128)S(1)} %convolution_bitcast_fusion.5), kind=kOutput, calls=%fused_computation.52 | convolution fusion | flops 402653184 | bytes 4456448 | tf_op jit(solution)/shard_map/ksc,qkc->qs/dot_general | solution.py:55
  24.3 1.1 copy.16
  25.4 1.2 pad_maximum_fusion.4
  26.6 1.5 copy.17
  28.0 1.9 collective-permute-start.2
  30.0 1.0 copy.18
  30.9 1.3 collective-permute-start.3
  32.2 0.7 and_convert_fusion
  33.0 0.7 slice.219
  35.2 1.2 copy.19
  36.3 2.0 copy.20
  38.4 0.9 maximum_bitcast_fusion
  39.5 1.7 pad_maximum_fusion
  41.5 5.5 %fusion.14 = f32[32,36,516]{2,1,0:T(8,128)S(1)} fusion(f32[33,38,518]{2,1,0:T(8,128)S(1)} %pad_maximum_fusion, f32[36,516]{1,0:T(8,128)S(1)} %copy-done.7, f32[36,516]{1,0:T(8,128)S(1)} %get-tuple-element.39, f32[36,516]{1,0:T(8,128)S(1)} %get-tuple-element.38), kind=kLoop, calls=%fused_computation.20 | loop fusion | flops 9510912 | bytes 24000192 | tf_op jit(solution)/shard_map/mul | solution.py:115
  46.9 1.5 fusion.37
  48.5 5.3 %fusion.4 = f32[32,34,514]{2,1,0:T(8,128)S(1)} fusion(f32[32,36,516]{2,1,0:T(8,128)S(1)} %fusion.14, f32[34,514]{1,0:T(8,128)S(1)} %copy-done.6, f32[34,514]{1,0:T(8,128)S(1)} %get-tuple-element.37, f32[34,514]{1,0:T(8,128)S(1)} %get-tuple-element.36), kind=kLoop, calls=%fused_computation.6 | loop fusion | flops 8947712 | bytes 22578992 | tf_op jit(solution)/shard_map/mul | solution.py:115
  53.8 1.5 fusion.34
  55.3 4.6 %convolution_bitcast_fusion.4 = f32[32,2,512]{2,1,0:T(2,128)S(1)} fusion(f32[32]{0:T(128)S(1)} %convert_bitcast_fusion, s32[32]{0:T(128)S(1)} %bitcast.221, f32[32,34,514]{2,1,0:T(8,128)S(1)} %fusion.4, f32[32,512]{1,0:T(8,128)S(1)} %copy-done.8, f32[32,512]{1,0:T(8,128)S(1)} %get-tuple-element.35, f32[32,512]{1,0:T(8,128)S(1)} %get-tuple-element.34), kind=kOutput, calls=%fused_computation.55 | convolution fusion | flops 20971648 | bytes 19203072 | tf_op jit(solution)/shard_map/rgk,qrgc->qkc/dot_general | solution.py:54
  60.0 4.5 %convolution_bitcast_fusion = f32[1,32,1024]{2,1,0:T(8,128)} fusion(f32[2,1024,512]{2,1,0:T(8,128)S(1)} %copy-done.2, f32[32,2,512]{2,1,0:T(2,128)S(1)} %convolution_bitcast_fusion.4), kind=kOutput, calls=%fused_computation.49 | convolution fusion | flops 402653184 | bytes 4456448 | tf_op jit(solution)/shard_map/ksc,qkc->qs/dot_general | solution.py:55
  64.5 4.5 %convolution_bitcast_fusion.1 = f32[1,32,1024]{2,1,0:T(8,128)} fusion(f32[2,1024,512]{2,1,0:T(8,128)S(1)} %copy-done.2, f32[32,2,512]{2,1,0:T(2,128)S(1)} %fusion.34), kind=kOutput, calls=%fused_computation.50 | convolution fusion | flops 402653184 | bytes 4456448 | tf_op jit(solution)/shard_map/ksc,qkc->qs/dot_general | solution.py:55
  69.1 4.5 %convolution_bitcast_fusion.2 = f32[1,32,1024]{2,1,0:T(8,128)} fusion(f32[2,1024,512]{2,1,0:T(8,128)S(1)} %copy-done.2, f32[32,2,512]{2,1,0:T(2,128)S(1)} %fusion.37), kind=kOutput, calls=%fused_computation.51 | convolution fusion | flops 402653184 | bytes 4456448 | tf_op jit(solution)/shard_map/ksc,qkc->qs/dot_general | solution.py:55
  73.6 135.0 %all-reduce.3.cloned.1.call-done = (f32[1,32,1024]{2,1,0:T(8,128)}, f32[1,32,1024]{2,1,0:T(8,128)}, f32[1,32,1024]{2,1,0:T(8,128)}, f32[32,1024]{1,0:T(8,128)}) async-done(((f32[1,32,1024]{2,1,0:T(8,128)}, f32[1,32,1024]{2,1,0:T(8,128)}, f32[1,32,1024]{2,1,0:T(8,128)}, f32[32,1024]{1,0:T(8,128)}), (f32[1,32,1024]{2,1,0:T(8,128)}, f32[1,32,1024]{2,1,0:T(8,128)}, f32[1,32,1024]{2,1,0:T(8,128)}, ...) | async-done | bytes 524304 | tf_op jit(solution)/shard_map/psum | solution.py:87
  208.6 1.1 pad_maximum_fusion.5
  209.7 2.2 convolution_bitcast_fusion.6
  212.6 3.6 %fusion.42 = f32[32,1,3]{2,1,0:T(1,128)S(1)} fusion(f32[3,32,1024]{2,1,0:T(8,128)S(1)} %pad_maximum_fusion.5, f32[32,1024,1]{1,0,2:T(8,128)} %bitcast.222), kind=kOutput, calls=%fused_computation.64 | convolution fusion | flops 1179648 | bytes 524672 | tf_op jit(solution)/shard_map/iqs,qs->iq/dot_general | solution.py:63
  216.5 2.2 fusion.40
  218.7 1.4 dynamic-slice_subtract_fusion
  220.1 17.2 %add_subtract_fusion = (f32[32,32,512]{2,1,0:T(8,128)}, f32[32,32,512]{2,1,0:T(8,128)}) fusion(f32[32,32,512]{2,1,0:T(8,128)} %param.5, f32[32,36,516]{2,1,0:T(8,128)S(1)} %fusion.14, f32[32,34,514]{2,1,0:T(8,128)} %copy-done, f32[32]{0:T(128)S(1)} %get-tuple-element.20, f32[32]{0:T(128)S(1)} %get-tuple-element.19, f32[32]{0:T(128)S(1)} %get-tuple-element.18, ...), kind=kLoop, calls=%fused_computation.43 | loop fusion | flops 14155776 | bytes 27459968 | tf_op jit(solution)/shard_map/sub | solution.py:133
  (49 shorter events, 4.5 us)
Async XLA Ops:
  7.2 8.5 %copy-start.1 = (f32[32,32,512]{2,1,0:T(8,128)S(1)}, f32[32,32,512]{2,1,0:T(8,128)}, u32[]{:S(2)}) copy-start(f32[32,32,512]{2,1,0:T(8,128)} %param.5) | copy-start | bytes 6291460
  7.2 8.4 %copy-start.10 = (s32[32,1]{0,1:T(1,128)S(1)}, s32[32,1]{0,1:T(1,128)}, u32[]{:S(2)}) copy-start(s32[32,1]{0,1:T(1,128)} %param.9) | copy-start | bytes 388
  7.2 8.5 %copy-start.9 = (s32[32,1]{0,1:T(1,128)S(1)}, s32[32,1]{0,1:T(1,128)}, u32[]{:S(2)}) copy-start(s32[32,1]{0,1:T(1,128)} %param.8) | copy-start | bytes 388
  7.2 201.4 %all-reduce.3.cloned.1.call-start = ((), (), s32[]{:S(2)}) async-start(), calls=%async_computation | async-start | bytes 1048576 | tf_op jit(solution)/shard_map/psum | solution.py:87
  8.8 15.3 %collective-permute-start = (f32[33,3,512]{2,0,1:T(8,128)S(1)}, f32[33,3,512]{2,0,1:T(8,128)S(1)}, u32[]{:S(2)}, u32[]{:S(2)}) collective-permute-start(f32[33,3,512]{2,0,1:T(8,128)S(1)} %copy.13), channel_id=1, source_target_pairs={{0,4},{4,8},{8,12},{12,16},{16,20},{20,24},{24,28},{1,5},{5,9},{9,... | collective-permute-start | bytes 608264 | tf_op jit(solution)/shard_map/ppermute | solution.py:20
  13.8 10.5 %collective-permute-start.1 = (f32[33,3,512]{2,0,1:T(8,128)S(1)}, f32[33,3,512]{2,0,1:T(8,128)}, u32[]{:S(2)}, u32[]{:S(2)}) collective-permute-start(f32[33,3,512]{2,0,1:T(8,128)S(1)} %copy.14), channel_id=1, source_target_pairs={{4,0},{8,4},{12,8},{16,12},{20,16},{24,20},{28,24},{5,1},{9,5},{13... | collective-permute-start | bytes 608264 | tf_op jit(solution)/shard_map/ppermute | solution.py:22
  16.8 8.6 %copy-start.5 = (f32[32,512]{1,0:T(8,128)S(1)}, f32[32,512]{1,0:T(8,128)}, u32[]{:S(2)}) copy-start(f32[32,512]{1,0:T(8,128)} %param.6) | copy-start | bytes 196612
  28.0 7.1 %collective-permute-start.2 = (f32[33,38,3]{1,0,2:T(8,128)S(1)}, f32[33,38,3]{1,0,2:T(8,128)}, u32[]{:S(2)}, u32[]{:S(2)}) collective-permute-start(f32[33,38,3]{1,0,2:T(8,128)S(1)} %copy.17), channel_id=1, source_target_pairs={{0,1},{1,2},{2,3},{4,5},{5,6},{6,7},{8,9},{9,10},{10,11},{12,13},{... | collective-permute-start | bytes 45152 | tf_op jit(solution)/shard_map/ppermute | solution.py:20
  30.9 5.4 %collective-permute-start.3 = (f32[33,38,3]{1,0,2:T(8,128)}, f32[33,38,3]{1,0,2:T(8,128)}, u32[]{:S(2)}, u32[]{:S(2)}) collective-permute-start(f32[33,38,3]{1,0,2:T(8,128)} %copy.18), channel_id=1, source_target_pairs={{1,0},{2,1},{3,2},{5,4},{6,5},{7,6},{9,8},{10,9},{11,10},{13,12},{... | collective-permute-start | bytes 45152 | tf_op jit(solution)/shard_map/ppermute | solution.py:22
  38.4 1.1 copy-start.3
  39.5 2.0 copy-start.7
  41.4 7.0 %copy-start.6 = (f32[34,514]{1,0:T(8,128)S(1)}, f32[34,514]{1,0:T(8,128)}, u32[]{:S(2)}) copy-start(f32[34,514]{1,0:T(8,128)} %slice.231) | copy-start | bytes 209716
  48.5 6.8 %copy-start.8 = (f32[32,512]{1,0:T(8,128)S(1)}, f32[32,512]{1,0:T(8,128)}, u32[]{:S(2)}) copy-start(f32[32,512]{1,0:T(8,128)} %slice.242) | copy-start | bytes 196612
  53.8 6.2 %copy-start = (f32[32,34,514]{2,1,0:T(8,128)}, f32[32,34,514]{2,1,0:T(8,128)S(1)}, u32[]{:S(2)}) copy-start(f32[32,34,514]{2,1,0:T(8,128)S(1)} %fusion.4) | copy-start | bytes 6710788
  55.3 4.7 %copy-start.2 = (f32[2,1024,512]{2,1,0:T(8,128)S(1)}, f32[2,1024,512]{2,1,0:T(8,128)}, u32[]{:S(2)}) copy-start(f32[2,1024,512]{2,1,0:T(8,128)} %param.7) | copy-start | bytes 12582916
  209.7 2.9 %copy-start.4 = (f32[3,32,1024]{2,1,0:T(8,128)}, f32[3,32,1024]{2,1,0:T(8,128)S(1)}, u32[]{:S(2)}) copy-start(f32[3,32,1024]{2,1,0:T(8,128)S(1)} %pad_maximum_fusion.5) | copy-start | bytes 1179652
Sparse Core Ops, SparseCore 0:
  73.8 134.8 all-reduce.2
where the time goes:
time: 245 us; the launch traced here: 244 us
  waiting for transfers between devices  136 us (56%)
  other arithmetic  37.4 us (15%)
  matrix products  37.1 us (15%)
  between operations  14.4 us (6%)
  local copies, waits for them, and re-layouts  10.2 us (4%)
  starting transfers between devices  9.41 us (4%)
    psum x1, waiting for transfers between devices, reduce_one(): return lax.psum(partial_sketch, ('gx', 'gy'))  135 us
    dot_general x4, matrix products, sketch_field(): jnp.einsum('ksc,qkc->qs', tiles, folded, precision=lax.Precision.HIGHEST)  20.3 us
    sub x1, other arithmetic, shards(): right_side - (coeff[0][:, None, None] * basis[1] + coeff[1][:, None, None...  17.2 us
    mul x2, other arithmetic, shards(): operate(current, absorb_wide[step:stop_row, step:stop_col])  10.7 us
    dot_general x4, matrix products, sketch_field(): jnp.einsum('rgk,qrgc->qkc', picker, blocks, precision=lax.Precision.HIGHEST)  8.79 us
    ppermute x2, starting transfers between devices, padded_2(): lax.ppermute(tail, axis, [(i, (i + 1) % count) for i in range(ends)])  6.8 us
  transfers between devices with their start and end apart: 5, of which 2 were waited for; matrix products, arithmetic and copies ran while one was open for 6% of the time, Pallas kernels for 0%

commit v1 on v0

v1 whole, which is shorter than its diff:
```python
import functools

import jax
import jax.numpy as jnp
from jax import lax
from jax.experimental import pallas as pl
from jax.experimental.pallas import tpu as pltpu
from jax.sharding import PartitionSpec as P

MESH = pl.DeviceIdType.MESH
DIAG = 2.4
RIDGE = 1e-05
HALO = 3
FULL = lax.Precision.HIGHEST


def kernel(
    ngx, ngy, rows, cols, width,
    x_ref, ab_ref, tiles_ref, w_ref,
    sol_ref, res_ref, skr_ref,
    v0, v1, v2, v3, inv, tl, packs, got, abh, fold, sk, part1, mid, part2, gath, gath1, gath2,
    sol_b, res_b,
    in_sem, out_sem, row_send, row_recv, col_send, col_recv, ab_send, ab_recv,
    s1s, s1r, s2s, s2r, g1s, g1r, g2s, g2r,
):
    gx = lax.axis_index("gx")
    gy = lax.axis_index("gy")
    ext = rows + 2 * HALO
    wide = cols + 128

    x_copy = pltpu.make_async_copy(x_ref, v0.at[HALO:HALO + rows, 0:32, 0:cols], in_sem.at[0])
    x_copy.start()
    t_copy = pltpu.make_async_copy(tiles_ref, tl, in_sem.at[1])
    t_copy.start()

    barrier = pltpu.get_barrier_semaphore()
    for k in range(1, ngx):
        pl.semaphore_signal(barrier, inc=1, device_id=(lax.rem(gx + k, ngx), gy), device_id_type=MESH)
    for k in range(1, ngy):
        pl.semaphore_signal(barrier, inc=1, device_id=(gx, lax.rem(gy + k, ngy)), device_id_type=MESH)
    up, down = gx > 0, gx < ngx - 1
    left, right = gy > 0, gy < ngy - 1
    there = {-1: up, 0: None, 1: down}
    side_there = (left, right)

    def both(a, b):
        return b if a is None else jnp.logical_and(a, b)

    for dx in (-1, 1):
        for side, dy in enumerate((-1, 1)):
            @pl.when(both(there[dx], side_there[side]))
            def _(dx=dx, dy=dy):
                pl.semaphore_signal(barrier, inc=1, device_id=(gx + dx, gy + dy), device_id_type=MESH)
    n_v = up.astype(jnp.int32) + down.astype(jnp.int32)
    n_h = left.astype(jnp.int32) + right.astype(jnp.int32)

    for r in range(rows):
        v0[HALO + r, 32:40, 0:cols] = jnp.broadcast_to(ab_ref[r:r + 1, :], (8, cols))
    x_copy.wait()

    lane = lax.broadcasted_iota(jnp.int32, (40, 128), 1)

    def pack(r, acc):
        here = (lane >= 4 * r) & (lane < 4 * r + 4)
        first = pltpu.roll(v0[HALO + r, :, 0:128], 4 * r, 1)
        last = pltpu.roll(v0[HALO + r, :, cols - 128:cols], lax.rem(4 * r + 4, 128), 1)
        return jnp.where(here, first, acc[0]), jnp.where(here, last, acc[1])

    zero = jnp.zeros((40, 128), jnp.float32)
    first, last = lax.fori_loop(0, rows, pack, (zero, zero))
    packs[0] = first
    packs[1] = last

    pl.semaphore_wait(barrier, ngx - 1 + ngy - 1 + n_v * n_h)

    row_copies = []
    for d, (dx, here) in enumerate(((-1, up), (1, down))):
        src = HALO if dx < 0 else rows
        dst = HALO + rows if dx < 0 else 0
        row_copies.append((pltpu.make_async_remote_copy(
            src_ref=v0.at[src:src + HALO, 0:32, 0:cols], dst_ref=v0.at[dst:dst + HALO, 0:32, 0:cols],
            send_sem=row_send.at[d], recv_sem=row_recv.at[d],
            device_id=(gx + dx, gy), device_id_type=MESH), here, (down, up)[d]))
        ar = 0 if dx < 0 else rows - 8
        row_copies.append((pltpu.make_async_remote_copy(
            src_ref=ab_ref.at[ar:ar + 8, :], dst_ref=abh.at[d],
            send_sem=ab_send.at[d], recv_sem=ab_recv.at[d],
            device_id=(gx + dx, gy), device_id_type=MESH), here, (down, up)[d]))
    col_copies = []
    for side, dy in enumerate((-1, 1)):
        for i, dx in enumerate((0, -1, 1)):
            slot = side * 3 + i
            to = both(there[dx], side_there[side])
            frm = both(there[-dx], side_there[1 - side])
            col_copies.append((pltpu.make_async_remote_copy(
                src_ref=packs.at[side], dst_ref=got.at[slot],
                send_sem=col_send.at[slot], recv_sem=col_recv.at[slot],
                device_id=(gx + dx, gy + dy), device_id_type=MESH), to, frm))
    for copy, to, frm in col_copies + row_copies:
        @pl.when(to)
        def _(copy=copy):
            copy.start()

    for d, frm in enumerate((down, up)):
        dst = HALO + rows if d == 0 else 0
        @pl.when(jnp.logical_not(frm))
        def _(d=d, dst=dst):
            v0[dst:dst + HALO, 0:32, 0:cols] = jnp.zeros((HALO, 32, cols), jnp.float32)
            abh[d] = jnp.zeros((8, cols), jnp.float32)
    for slot, (copy, to, frm) in enumerate(col_copies):
        @pl.when(jnp.logical_not(frm))
        def _(slot=slot):
            got[slot] = jnp.zeros((40, 128), jnp.float32)

    for copy, to, frm in col_copies + row_copies:
        @pl.when(frm)
        def _(copy=copy):
            copy.wait_recv()

    for i in range(HALO):
        v0[i, 32:40, 0:cols] = jnp.broadcast_to(abh[1, 8 - HALO + i:8 - HALO + i + 1, :], (8, cols))
        v0[HALO + rows + i, 32:40, 0:cols] = jnp.broadcast_to(abh[0, i:i + 1, :], (8, cols))

    def unpack(slot_right, slot_left, r, dest):
        a = pltpu.roll(got[slot_right], lax.rem(128 - 4 * r, 128), 1)
        b = pltpu.roll(got[slot_left], lax.rem(252 - 4 * r, 128), 1)
        v0[dest, :, cols:wide] = jnp.where(lane < 4, a, jnp.where(lane >= 124, b, 0.0))

    def unpack_own(r, c):
        unpack(0, 3, r, HALO + r)
        return c

    lax.fori_loop(0, rows, unpack_own, 0)
    for i in range(HALO):
        unpack(1, 4, i, HALO + rows + i)
        unpack(2, 5, rows - HALO + i, i)

    lane_w = lax.broadcasted_iota(jnp.int32, (8, wide), 1)
    col_in = (lane_w < cols) | ((lane_w < cols + HALO) & right) | ((lane_w >= wide - HALO) & left)

    def make_inv(r, c):
        row = gx * rows + r - HALO
        ok = col_in & (row >= 0) & (row < rows * ngx)
        inv[r] = jnp.where(ok, 1.0 / (DIAG + v0[r, 32:40, :]), 0.0)
        return c

    lax.fori_loop(0, ext, make_inv, 0)

    def step(src, dst, n, lo, hi):
        for t in range(4):
            q = slice(8 * t, 8 * t + 8)

            def parts(r):
                v = src[r, q, :]
                e = pltpu.roll(v, wide - 1, 1)
                w = pltpu.roll(v, 1, 1)
                return v, e + w, e - w

            vp, _, dp = parts(lo - 1)
            up0 = 0.2 * vp + 0.15 * dp
            z = jnp.zeros((8, cols), jnp.float32)

            def body(r, carry):
                upv, v, s, d, a0, a1, b0, b1 = carry
                vn, sn, dn = parts(r + 1)
                out = v - inv[r] * (s + upv + (0.2 * vn - 0.15 * dn))
                dst[r, q, :] = out
                o = out[:, 0:cols]
                a0 = a0 + w_ref[0, r] * o
                a1 = a1 + w_ref[1, r] * o
                if n == 1:
                    b0 = b0 + w_ref[0, r] * v[:, 0:cols]
                    b1 = b1 + w_ref[1, r] * v[:, 0:cols]
                return 0.2 * v + 0.15 * d, vn, sn, dn, a0, a1, b0, b1

            v, s, d = parts(lo)
            _, _, _, _, a0, a1, b0, b1 = lax.fori_loop(lo, hi, body, (up0, v, s, d, z, z, z, z))
            fold[0, 32 * n + 8 * t:32 * n + 8 * t + 8, :] = a0
            fold[1, 32 * n + 8 * t:32 * n + 8 * t + 8, :] = a1
            if n == 1:
                fold[0, q, :] = b0
                fold[1, q, :] = b1

    step(v0, v1, 1, 1, ext - 1)
    step(v1, v2, 2, 2, ext - 2)
    step(v2, v3, 3, 3, ext - 3)
    t_copy.wait()

    block = ngy * width

    def mm(g, c):
        rows_g = pl.ds(pl.multiple_of(g * block, block), block)
        out = jnp.zeros((block, 128), jnp.float32)
        for k in range(2):
            out = out + lax.dot_general(
                tl[k, rows_g, :], fold[k], (((1,), (1,)), ((), ())),
                precision=FULL, preferred_element_type=jnp.float32)
        for j in range(ngy):
            sk[j, g] = out[j * width:(j + 1) * width, :]
        return c

    lax.fori_loop(0, ngx, mm, 0)

    def exchange(n, axis, pick, land, ss, rs):
        me = gx if axis == 0 else gy
        out = []
        for k in range(1, n):
            peer = lax.rem(me + k, n)
            out.append(pltpu.make_async_remote_copy(
                src_ref=pick(peer), dst_ref=land.at[k - 1], send_sem=ss.at[k - 1], recv_sem=rs.at[k - 1],
                device_id=(peer, gy) if axis == 0 else (gx, peer), device_id_type=MESH))
        for c in out:
            c.start()
        return out

    c1 = exchange(ngy, 1, lambda p: sk.at[p], part1, s1s, s1r)
    total = sk[gy]
    for k, c in enumerate(c1):
        c.wait_recv()
        total = total + part1[k]
    mid[...] = total
    c2 = exchange(ngx, 0, lambda p: mid.at[p], part2, s2s, s2r)
    own = mid[gx]
    for k, c in enumerate(c2):
        c.wait_recv()
        own = own + part2[k]

    prods = [jnp.sum(own * own, 0, keepdims=True)]
    for k in (1, 2):
        prods.append(jnp.sum(own * pltpu.roll(own, 32 * k, 1), 0, keepdims=True))
    gath[0] = jnp.concatenate(prods + [jnp.zeros((5, 128), jnp.float32)], 0)
    c3 = exchange(ngy, 1, lambda p: gath.at[0], gath1, g1s, g1r)
    tot = gath[0]
    for k, c in enumerate(c3):
        c.wait_recv()
        tot = tot + gath1[k]
    gath[1] = tot
    c4 = exchange(ngx, 0, lambda p: gath.at[1], gath2, g2s, g2r)
    for k, c in enumerate(c4):
        c.wait_recv()
        tot = tot + gath2[k]

    by = [tot] + [pltpu.roll(tot, 128 - 32 * f, 1) for f in (1, 2, 3)]

    def at(k, f):
        return by[f][k:k + 1, :]

    g00, g11, g22 = at(0, 1), at(0, 2), at(0, 3)
    g10, g21, g20 = at(1, 2), at(1, 3), at(2, 3)
    h0, h1, h2 = at(1, 1), at(2, 2), at(1, 0)
    ridge = RIDGE * (g00 + g11 + g22)
    p0 = jnp.sqrt(g00 + ridge)
    l10 = g10 / p0
    l20 = g20 / p0
    p1 = jnp.sqrt(g11 + ridge - l10 * l10)
    l21 = (g21 - l20 * l10) / p1
    p2 = jnp.sqrt(g22 + ridge - l20 * l20 - l21 * l21)
    f0 = h0 / p0
    f1 = (h1 - l10 * f0) / p1
    f2 = (h2 - l20 * f0 - l21 * f1) / p2
    y2 = f2 / p2
    y1 = (f1 - l21 * y2) / p1
    y0 = (f0 - l10 * y1 - l20 * y2) / p0

    skr_ref[...] = own - (y0 * pltpu.roll(own, 96, 1) + y1 * pltpu.roll(own, 64, 1) + y2 * pltpu.roll(own, 32, 1))

    same = lax.broadcasted_iota(jnp.int32, (32, 128), 0) == lax.broadcasted_iota(jnp.int32, (32, 128), 1)
    c0, c1_, c2_ = [
        jnp.sum(jnp.where(same, jnp.broadcast_to(y, (32, 128)), 0.0), 1, keepdims=True) for y in (y0, y1, y2)
    ]

    n_out = 4
    each = rows // n_out
    outs = []
    for b in range(n_out):
        def combine(r, c, b=b):
            for t in range(4):
                q = slice(8 * t, 8 * t + 8)
                k0, k1, k2 = c0[q], c1_[q], c2_[q]
                a, bb, cc, dd = [v[HALO + r, q, 0:cols] for v in (v0, v1, v2, v3)]
                sol_b[r, q, :] = k0 * a + k1 * bb + k2 * cc
                res_b[r, q, :] = a - (k0 * bb + k1 * cc + k2 * dd)
            return c

        lax.fori_loop(b * each, (b + 1) * each, combine, 0)
        for o, (buf, ref) in enumerate(((sol_b, sol_ref), (res_b, res_ref))):
            part = slice(b * each, (b + 1) * each)
            oc = pltpu.make_async_copy(buf.at[part], ref.at[part], out_sem.at[2 * b + o])
            oc.start()
            outs.append(oc)

    for copy, to, frm in col_copies + row_copies:
        @pl.when(to)
        def _(copy=copy):
            copy.wait_send()
    for c in c1 + c2 + c3 + c4:
        c.wait_send()
    for oc in outs:
        oc.wait()


def shards(ngx, ngy, right_side, absorb, tiles, tile_index, tile_sign):
    count, rows, cols = right_side.shape
    sketch = tiles.shape[1]
    width = sketch // (ngx * ngy)
    ext, wide = rows + 2 * HALO, cols + 128
    which = jnp.arange(tiles.shape[0], dtype=jnp.int32)[:, None]
    weights = jnp.where(tile_index[:, 0][None] == which, (2 * tile_sign[:, 0] - 1)[None], 0).astype(jnp.float32)
    weights = jnp.pad(weights, ((0, 0), (HALO, HALO)))
    f32 = jnp.float32
    dma = pltpu.SemaphoreType.DMA
    any_spec = pl.BlockSpec(memory_space=pl.ANY)
    vmem_spec = pl.BlockSpec(memory_space=pltpu.VMEM)
    sol, res, skr = pl.pallas_call(
        functools.partial(kernel, ngx, ngy, rows, cols, width),
        out_shape=(
            jax.ShapeDtypeStruct((rows, count, cols), f32),
            jax.ShapeDtypeStruct((rows, count, cols), f32),
            jax.ShapeDtypeStruct((width, 128), f32),
        ),
        in_specs=[any_spec, vmem_spec, any_spec, pl.BlockSpec(memory_space=pltpu.SMEM)],
        out_specs=(any_spec, any_spec, vmem_spec),
        scratch_shapes=[
            pltpu.VMEM((ext, 40, wide), f32),
            pltpu.VMEM((ext, 32, wide), f32),
            pltpu.VMEM((ext, 32, wide), f32),
            pltpu.VMEM((ext, 32, wide), f32),
            pltpu.VMEM((ext, 8, wide), f32),
            pltpu.VMEM(tiles.shape, f32),
            pltpu.VMEM((2, 40, 128), f32),
            pltpu.VMEM((6, 40, 128), f32),
            pltpu.VMEM((2, 8, cols), f32),
            pltpu.VMEM((2, 128, cols), f32),
            pltpu.VMEM((ngy, ngx, width, 128), f32),
            pltpu.VMEM((ngy - 1, ngx, width, 128), f32),
            pltpu.VMEM((ngx, width, 128), f32),
            pltpu.VMEM((ngx - 1, width, 128), f32),
            pltpu.VMEM((2, 8, 128), f32),
            pltpu.VMEM((ngy - 1, 8, 128), f32),
            pltpu.VMEM((ngx - 1, 8, 128), f32),
            pltpu.VMEM((rows, count, cols), f32),
            pltpu.VMEM((rows, count, cols), f32),
            dma((2,)), dma((8,)), dma((2,)), dma((2,)), dma((6,)), dma((6,)), dma((2,)), dma((2,)),
            dma((ngy - 1,)), dma((ngy - 1,)), dma((ngx - 1,)), dma((ngx - 1,)),
            dma((ngy - 1,)), dma((ngy - 1,)), dma((ngx - 1,)), dma((ngx - 1,)),
        ],
        compiler_params=pltpu.CompilerParams(
            collective_id=0, has_side_effects=True, vmem_limit_bytes=56 * 2**20
        ),
    )(jnp.transpose(right_side, (1, 0, 2)), absorb, tiles, weights)
    return jnp.transpose(sol, (1, 0, 2)), jnp.transpose(res, (1, 0, 2)), skr[:, :count].T


def solution(mesh):
    in_specs = (P(None, "gx", "gy"), P("gx", "gy"), P(), P("gx", "gy"), P("gx", "gy"))
    out_specs = (P(None, "gx", "gy"), P(None, "gx", "gy"), P(None, ("gx", "gy")))
    fn = functools.partial(shards, mesh.shape["gx"], mesh.shape["gy"])
    return jax.shard_map(fn, mesh=mesh, in_specs=in_specs, out_specs=out_specs, check_vma=False)
```

time: 245 us -> 100 us (0.41)
  waiting for transfers between devices: 136 us -> 0 us
  Pallas kernels: 0 us -> 85.8 us
  matrix products: 37.1 us -> 0 us
  other arithmetic: 37.4 us -> 1.32 us
  between operations: 14.4 us -> 0.65 us
  starting transfers between devices: 9.41 us -> 0 us
    psum x1 -> x0, waiting for transfers between devices: 135 us -> none  [reduce_one(): return lax.psum(partial_sketch, ('gx', 'gy'))]
    pallas_call x0 -> x1, Pallas kernels: none -> 85.8 us  [shards(): pl.pallas_call(functools.partial(kernel, ngx, ngy, rows, cols, width), ou...]
    dot_general x11 -> x0, matrix products: 37.1 us -> none  [the longest x4 20.3 us: sketch_field(): jnp.einsum('ksc,qkc->qs', tiles, folded, precision=lax.Precision.HIGHEST)]
    sub x2 -> x1, other arithmetic: 18.6 us -> 0.66 us  [shards(): 2 * tile_sign[:, 0] - 1]
    unnamed x22 -> x8, local copies, waits for them, and re-layouts: 0.25 us -> 11.6 us
    mul x3 -> x0, other arithmetic: 10.7 us -> none  [the longest x2 10.7 us: shards(): operate(current, absorb_wide[step:stop_row, step:stop_col])]
    ppermute x4 -> x0, starting transfers between devices: 9.37 us -> none  [the longest x2 6.8 us: padded_2(): lax.ppermute(tail, axis, [(i, (i + 1) % count) for i in range(ends)])]
    slice x8 -> x0, local copies, waits for them, and re-layouts: 5.38 us -> none  [the longest x3 2.17 us: shards(): inside_grid[step:stop_row, step:stop_col]]
  transfers between devices with their start and end apart: 5 -> 0, of which waited for: 2 -> 0; matrix products, arithmetic and copies ran while one was open for 6% -> 0% of each run, Pallas kernels for 0% -> 0%
where the time goes in v1:
time: 100 us
  Pallas kernels  85.8 us (86%)
  local copies, waits for them, and re-layouts  12.3 us (12%)
  other arithmetic  1.32 us (1%)
    pallas_call x1, Pallas kernels, shards(): pl.pallas_call(functools.partial(kernel, ngx, ngy, rows, cols, width), ou...  85.8 us
    unnamed x8, local copies, waits for them, and re-layouts  11.6 us

profile of v1, /device:TPU:0, one launch (start us, length us, event | category | flops | bytes accessed | tf_op | source)
XLA Modules:
  0.0 100.0 jit_solution(4690767531043081732)
XLA Ops:
  0.6 0.7 add_bitcast_fusion
  1.3 0.7 fusion
  1.9 0.6 pad.4.w_ref
  2.6 4.1 %copy.13 = f32[32,32,512]{2,0,1:T(8,128)} copy(f32[32,32,512]{2,1,0:T(8,128)} %param.5) | data formatting | bytes 4194304 | tf_op args[0]
  6.7 85.8 %shard_map.76 = (f32[32,32,512]{2,1,0:T(8,128)}, f32[32,32,512]{2,1,0:T(8,128)}, f32[32,128]{1,0:T(8,128)}) custom-call(f32[32,32,512]{2,1,0:T(8,128)} %bitcast.10, f32[32,512]{1,0:T(8,128)} %ab_ref.1, f32[2,1024,512]{2,1,0:T(8,128)} %tiles_ref.1, f32[2,38]{1,0:T(2,128)} %pad.4.w_ref), custom_call_target="tpu_custom_call" | custom-call | tf_op jit(solution)/shard_map/pallas_call | solution.py:314
  92.5 0.0 copy-start
  92.5 4.3 %copy.9 = f32[32,32,512]{2,1,0:T(8,128)} copy(f32[32,32,512]{2,0,1:T(8,128)} %bitcast.12) | data formatting | bytes 4194304
  96.8 0.0 copy-done
  96.8 0.0 copy-start.1
  96.8 2.5 %copy.10 = f32[32,32,512]{2,1,0:T(8,128)} copy(f32[32,32,512]{2,0,1:T(8,128)S(1)} %bitcast.11) | data formatting | bytes 4194304
  99.3 0.0 copy-done.1
  99.3 0.7 copy.11
  (1 shorter events, 0.0 us)
Async XLA Ops:
  92.5 4.3 %copy-start = (f32[32,32,512]{2,1,0:T(8,128)S(1)}, f32[32,32,512]{2,1,0:T(8,128)}, u32[]{:S(2)}) copy-start(f32[32,32,512]{2,1,0:T(8,128)} %get-tuple-element.7) | copy-start | bytes 6291460
  96.8 2.5 %copy-start.1 = (f32[32,128]{1,0:T(8,128)S(1)}, f32[32,128]{1,0:T(8,128)}, u32[]{:S(2)}) copy-start(f32[32,128]{1,0:T(8,128)} %get-tuple-element.8) | copy-start | bytes 49156

commit v2 on v1

--- a/solution.py
+++ b/solution.py
@@ -11,15 +11,15 @@
 DIAG = 2.4
 RIDGE = 1e-05
 HALO = 3
-FULL = lax.Precision.HIGHEST
+UNROLL = 14
 
 
 def kernel(
     ngx, ngy, rows, cols, width,
-    x_ref, ab_ref, tiles_ref, w_ref,
-    sol_ref, res_ref, skr_ref,
+    x_ref, ab_ref, tiles_ref, index_ref, sign_ref,
+    basis_ref, y_ref, skr_ref,
     v0, v1, v2, v3, inv, tl, packs, got, abh, fold, sk, part1, mid, part2, gath, gath1, gath2,
-    sol_b, res_b,
+    w_ref,
     in_sem, out_sem, row_send, row_recv, col_send, col_recv, ab_send, ab_recv,
     s1s, s1r, s2s, s2r, g1s, g1r, g2s, g2r,
 ):
@@ -29,7 +29,8 @@
     wide = cols + 128
 
     x_copy = pltpu.make_async_copy(x_ref, v0.at[HALO:HALO + rows, 0:32, 0:cols], in_sem.at[0])
-    x_copy.start()
+    for r in range(rows):
+        pltpu.make_async_copy(x_ref.at[:, r, :], v0.at[HALO + r, 0:32, 0:cols], in_sem.at[0]).start()
     t_copy = pltpu.make_async_copy(tiles_ref, tl, in_sem.at[1])
     t_copy.start()
 
@@ -53,6 +54,15 @@
                 pl.semaphore_signal(barrier, inc=1, device_id=(gx + dx, gy + dy), device_id_type=MESH)
     n_v = up.astype(jnp.int32) + down.astype(jnp.int32)
     n_h = left.astype(jnp.int32) + right.astype(jnp.int32)
+
+    for r in range(ext):
+        if HALO <= r < HALO + rows:
+            sign = (2 * sign_ref[r - HALO] - 1).astype(jnp.float32)
+            for k in range(2):
+                w_ref[k, r] = jnp.where(index_ref[r - HALO] == k, sign, 0.0)
+        else:
+            w_ref[0, r] = 0.0
+            w_ref[1, r] = 0.0
 
     for r in range(rows):
         v0[HALO + r, 32:40, 0:cols] = jnp.broadcast_to(ab_ref[r:r + 1, :], (8, cols))
@@ -112,41 +122,53 @@
         def _(slot=slot):
             got[slot] = jnp.zeros((40, 128), jnp.float32)
 
-    for copy, to, frm in col_copies + row_copies:
-        @pl.when(frm)
-        def _(copy=copy):
-            copy.wait_recv()
-
-    for i in range(HALO):
-        v0[i, 32:40, 0:cols] = jnp.broadcast_to(abh[1, 8 - HALO + i:8 - HALO + i + 1, :], (8, cols))
-        v0[HALO + rows + i, 32:40, 0:cols] = jnp.broadcast_to(abh[0, i:i + 1, :], (8, cols))
+    z = jnp.zeros((8, cols), jnp.float32)
+    for t in range(4):
+        q0 = slice(8 * t, 8 * t + 8)
+
+        def fold_rows(r, acc, q0=q0):
+            a0, a1 = acc
+            for u in range(4):
+                o = v0[r * 4 + u + HALO, q0, 0:cols]
+                a0 = a0 + w_ref[0, r * 4 + u + HALO] * o
+                a1 = a1 + w_ref[1, r * 4 + u + HALO] * o
+            return a0, a1
+
+        a0, a1 = lax.fori_loop(0, rows // 4, fold_rows, (z, z))
+        fold[0, q0, :] = a0
+        fold[1, q0, :] = a1
+
+    def wait_recv(copies):
+        for copy, to, frm in copies:
+            @pl.when(frm)
+            def _(copy=copy):
+                copy.wait_recv()
+
+    wait_recv([col_copies[0], col_copies[3]])
 
     def unpack(slot_right, slot_left, r, dest):
         a = pltpu.roll(got[slot_right], lax.rem(128 - 4 * r, 128), 1)
         b = pltpu.roll(got[slot_left], lax.rem(252 - 4 * r, 128), 1)
         v0[dest, :, cols:wide] = jnp.where(lane < 4, a, jnp.where(lane >= 124, b, 0.0))
 
-    def unpack_own(r, c):
-        unpack(0, 3, r, HALO + r)
-        return c
-
-    lax.fori_loop(0, rows, unpack_own, 0)
-    for i in range(HALO):
-        unpack(1, 4, i, HALO + rows + i)
-        unpack(2, 5, rows - HALO + i, i)
-
     lane_w = lax.broadcasted_iota(jnp.int32, (8, wide), 1)
     col_in = (lane_w < cols) | ((lane_w < cols + HALO) & right) | ((lane_w >= wide - HALO) & left)
 
-    def make_inv(r, c):
+    def make_inv(r):
         row = gx * rows + r - HALO
         ok = col_in & (row >= 0) & (row < rows * ngx)
         inv[r] = jnp.where(ok, 1.0 / (DIAG + v0[r, 32:40, :]), 0.0)
+
+    def unpack_own(r, c):
+        for u in range(4):
+            unpack(0, 3, 4 * r + u, HALO + 4 * r + u)
+        for u in range(4):
+            make_inv(HALO + 4 * r + u)
         return c
 
-    lax.fori_loop(0, ext, make_inv, 0)
-
-    def step(src, dst, n, lo, hi):
+    lax.fori_loop(0, rows // 4, unpack_own, 0)
+
+    def step(src, dst, n, lo, hi, unroll, fresh):
         for t in range(4):
             q = slice(8 * t, 8 * t + 8)
 
@@ -158,43 +180,75 @@
 
             vp, _, dp = parts(lo - 1)
             up0 = 0.2 * vp + 0.15 * dp
-            z = jnp.zeros((8, cols), jnp.float32)
-
-            def body(r, carry):
-                upv, v, s, d, a0, a1, b0, b1 = carry
+
+            def row(r, carry):
+                upv, v, s, d, a0, a1 = carry
                 vn, sn, dn = parts(r + 1)
                 out = v - inv[r] * (s + upv + (0.2 * vn - 0.15 * dn))
                 dst[r, q, :] = out
                 o = out[:, 0:cols]
                 a0 = a0 + w_ref[0, r] * o
                 a1 = a1 + w_ref[1, r] * o
-                if n == 1:
-                    b0 = b0 + w_ref[0, r] * v[:, 0:cols]
-                    b1 = b1 + w_ref[1, r] * v[:, 0:cols]
-                return 0.2 * v + 0.15 * d, vn, sn, dn, a0, a1, b0, b1
+                return 0.2 * v + 0.15 * d, vn, sn, dn, a0, a1
+
+            def body(i, carry):
+                for u in range(unroll):
+                    carry = row(lo + i * unroll + u, carry)
+                return carry
 
             v, s, d = parts(lo)
-            _, _, _, _, a0, a1, b0, b1 = lax.fori_loop(lo, hi, body, (up0, v, s, d, z, z, z, z))
-            fold[0, 32 * n + 8 * t:32 * n + 8 * t + 8, :] = a0
-            fold[1, 32 * n + 8 * t:32 * n + 8 * t + 8, :] = a1
-            if n == 1:
-                fold[0, q, :] = b0
-                fold[1, q, :] = b1
-
-    step(v0, v1, 1, 1, ext - 1)
-    step(v1, v2, 2, 2, ext - 2)
-    step(v2, v3, 3, 3, ext - 3)
+            fq = slice(32 * n + 8 * t, 32 * n + 8 * t + 8)
+            start = (z, z) if fresh else (fold[0, fq, :], fold[1, fq, :])
+            carry = (up0, v, s, d) + start
+            trips = (hi - lo) // unroll
+            if trips > 1:
+                carry = lax.fori_loop(0, trips, body, carry)
+            else:
+                carry = body(0, carry)
+            for r in range(lo + trips * unroll, hi):
+                carry = row(r, carry)
+            fold[0, fq, :] = carry[4]
+            fold[1, fq, :] = carry[5]
+
+    for n, (src, dst) in enumerate(((v0, v1), (v1, v2), (v2, v3)), 1):
+        step(src, dst, n, HALO + n, ext - HALO - n, UNROLL, True)
+
+    wait_recv(col_copies[1:3] + col_copies[4:] + row_copies)
+    for i in range(HALO):
+        v0[i, 32:40, 0:cols] = jnp.broadcast_to(abh[1, 8 - HALO + i:8 - HALO + i + 1, :], (8, cols))
+        v0[HALO + rows + i, 32:40, 0:cols] = jnp.broadcast_to(abh[0, i:i + 1, :], (8, cols))
+        unpack(1, 4, i, HALO + rows + i)
+        unpack(2, 5, rows - HALO + i, i)
+    for i in range(HALO):
+        make_inv(i)
+        make_inv(HALO + rows + i)
+    for n, (src, dst) in enumerate(((v0, v1), (v1, v2), (v2, v3)), 1):
+        step(src, dst, n, n, HALO + n, HALO, False)
+        step(src, dst, n, ext - HALO - n, ext - n, HALO, False)
+    out_copies = []
+    for n, v in enumerate((v1, v2, v3)):
+        for r in range(rows):
+            pltpu.make_async_copy(v.at[HALO + r, :, 0:cols], basis_ref.at[n, :, r, :], out_sem.at[n]).start()
+        out_copies.append(pltpu.make_async_copy(v.at[HALO:HALO + rows, :, 0:cols], basis_ref.at[n], out_sem.at[n]))
     t_copy.wait()
 
     block = ngy * width
+
+    def halves(a):
+        hi = a.astype(jnp.bfloat16)
+        return hi, (a - hi.astype(jnp.float32)).astype(jnp.bfloat16)
+
+    fold_hi, fold_lo = zip(*[halves(fold[k]) for k in range(2)])
+
+    def nt(a, b):
+        return lax.dot_general(a, b, (((1,), (1,)), ((), ())), preferred_element_type=jnp.float32)
 
     def mm(g, c):
         rows_g = pl.ds(pl.multiple_of(g * block, block), block)
         out = jnp.zeros((block, 128), jnp.float32)
         for k in range(2):
-            out = out + lax.dot_general(
-                tl[k, rows_g, :], fold[k], (((1,), (1,)), ((), ())),
-                precision=FULL, preferred_element_type=jnp.float32)
+            hi, lo = halves(tl[k, rows_g, :])
+            out = out + (nt(hi, fold_hi[k]) + (nt(hi, fold_lo[k]) + nt(lo, fold_hi[k])))
         for j in range(ngy):
             sk[j, g] = out[j * width:(j + 1) * width, :]
         return c
@@ -264,30 +318,7 @@
 
     skr_ref[...] = own - (y0 * pltpu.roll(own, 96, 1) + y1 * pltpu.roll(own, 64, 1) + y2 * pltpu.roll(own, 32, 1))
 
-    same = lax.broadcasted_iota(jnp.int32, (32, 128), 0) == lax.broadcasted_iota(jnp.int32, (32, 128), 1)
-    c0, c1_, c2_ = [
-        jnp.sum(jnp.where(same, jnp.broadcast_to(y, (32, 128)), 0.0), 1, keepdims=True) for y in (y0, y1, y2)
-    ]
-
-    n_out = 4
-    each = rows // n_out
-    outs = []
-    for b in range(n_out):
-        def combine(r, c, b=b):
-            for t in range(4):
-                q = slice(8 * t, 8 * t + 8)
-                k0, k1, k2 = c0[q], c1_[q], c2_[q]
-                a, bb, cc, dd = [v[HALO + r, q, 0:cols] for v in (v0, v1, v2, v3)]
-                sol_b[r, q, :] = k0 * a + k1 * bb + k2 * cc
-                res_b[r, q, :] = a - (k0 * bb + k1 * cc + k2 * dd)
-            return c
-
-        lax.fori_loop(b * each, (b + 1) * each, combine, 0)
-        for o, (buf, ref) in enumerate(((sol_b, sol_ref), (res_b, res_ref))):
-            part = slice(b * each, (b + 1) * each)
-            oc = pltpu.make_async_copy(buf.at[part], ref.at[part], out_sem.at[2 * b + o])
-            oc.start()
-            outs.append(oc)
+    y_ref[...] = jnp.concatenate([y0, y1, y2, jnp.zeros((5, 128), jnp.float32)], 0)
 
     for copy, to, frm in col_copies + row_copies:
         @pl.when(to)
@@ -295,7 +326,7 @@
             copy.wait_send()
     for c in c1 + c2 + c3 + c4:
         c.wait_send()
-    for oc in outs:
+    for oc in out_copies:
         oc.wait()
 
 
@@ -304,22 +335,19 @@
     sketch = tiles.shape[1]
     width = sketch // (ngx * ngy)
     ext, wide = rows + 2 * HALO, cols + 128
-    which = jnp.arange(tiles.shape[0], dtype=jnp.int32)[:, None]
-    weights = jnp.where(tile_index[:, 0][None] == which, (2 * tile_sign[:, 0] - 1)[None], 0).astype(jnp.float32)
-    weights = jnp.pad(weights, ((0, 0), (HALO, HALO)))
     f32 = jnp.float32
     dma = pltpu.SemaphoreType.DMA
     any_spec = pl.BlockSpec(memory_space=pl.ANY)
     vmem_spec = pl.BlockSpec(memory_space=pltpu.VMEM)
-    sol, res, skr = pl.pallas_call(
+    basis, y, skr = pl.pallas_call(
         functools.partial(kernel, ngx, ngy, rows, cols, width),
         out_shape=(
-            jax.ShapeDtypeStruct((rows, count, cols), f32),
-            jax.ShapeDtypeStruct((rows, count, cols), f32),
+            jax.ShapeDtypeStruct((3, count, rows, cols), f32),
+            jax.ShapeDtypeStruct((8, 128), f32),
             jax.ShapeDtypeStruct((width, 128), f32),
         ),
-        in_specs=[any_spec, vmem_spec, any_spec, pl.BlockSpec(memory_space=pltpu.SMEM)],
-        out_specs=(any_spec, any_spec, vmem_spec),
+        in_specs=[any_spec, vmem_spec, any_spec] + [pl.BlockSpec(memory_space=pltpu.SMEM)] * 2,
+        out_specs=(any_spec, vmem_spec, vmem_spec),
         scratch_shapes=[
             pltpu.VMEM((ext, 40, wide), f32),
             pltpu.VMEM((ext, 32, wide), f32),
@@ -338,17 +366,19 @@
             pltpu.VMEM((2, 8, 128), f32),
             pltpu.VMEM((ngy - 1, 8, 128), f32),
             pltpu.VMEM((ngx - 1, 8, 128), f32),
-            pltpu.VMEM((rows, count, cols), f32),
-            pltpu.VMEM((rows, count, cols), f32),
-            dma((2,)), dma((8,)), dma((2,)), dma((2,)), dma((6,)), dma((6,)), dma((2,)), dma((2,)),
+            pltpu.SMEM((2, ext), f32),
+            dma((2,)), dma((3,)), dma((2,)), dma((2,)), dma((6,)), dma((6,)), dma((2,)), dma((2,)),
             dma((ngy - 1,)), dma((ngy - 1,)), dma((ngx - 1,)), dma((ngx - 1,)),
             dma((ngy - 1,)), dma((ngy - 1,)), dma((ngx - 1,)), dma((ngx - 1,)),
         ],
         compiler_params=pltpu.CompilerParams(
             collective_id=0, has_side_effects=True, vmem_limit_bytes=56 * 2**20
         ),
-    )(jnp.transpose(right_side, (1, 0, 2)), absorb, tiles, weights)
-    return jnp.transpose(sol, (1, 0, 2)), jnp.transpose(res, (1, 0, 2)), skr[:, :count].T
+    )(right_side, absorb, tiles, tile_index[:, 0], tile_sign[:, 0])
+    c0, c1, c2 = [y[k, :count, None, None] for k in range(3)]
+    solved = c0 * right_side + c1 * basis[0] + c2 * basis[1]
+    left_over = right_side - (c0 * basis[0] + c1 * basis[1] + c2 * basis[2])
+    return solved, left_over, skr[:, :count].T
 
 
 def solution(mesh):

time: 100 us -> 52.6 us (0.53)
  Pallas kernels: 85.8 us -> 43.8 us
  local copies, waits for them, and re-layouts: 12.3 us -> 1.49 us
  other arithmetic: 1.32 us -> 6.47 us
    pallas_call x1, Pallas kernels: 85.8 us -> 43.8 us  [shards(): pl.pallas_call(functools.partial(kernel, ngx, ngy, rows, cols, width), ou...]
    unnamed x8 -> x5, local copies, waits for them, and re-layouts: 11.6 us -> 0.69 us
    sub x1, other arithmetic: 0.66 us -> 6.47 us  [shards(): left_over = right_side - (c0 * basis[0] + c1 * basis[1] + c2 * basis[2])]
where the time goes in v2:
time: 52.6 us; the launch traced here: 52.4 us
  Pallas kernels  43.8 us (83%)
  other arithmetic  6.47 us (12%)
  local copies, waits for them, and re-layouts  1.49 us (3%)
  between operations  0.65 us (1%)
    pallas_call x1, Pallas kernels, shards(): pl.pallas_call(functools.partial(kernel, ngx, ngy, rows, cols, width), ou...  43.8 us
    sub x1, other arithmetic, shards(): left_over = right_side - (c0 * basis[0] + c1 * basis[1] + c2 * basis[2])  6.47 us

profile of v2, /device:TPU:0, one launch (start us, length us, event | category | flops | bytes accessed | tf_op | source)
XLA Modules:
  0.0 52.4 jit_solution(9291282441860188491)
XLA Ops:
  0.6 0.0 copy-start
  0.6 43.8 %shard_map.76 = (f32[3,32,32,512]{3,2,1,0:T(8,128)}, f32[8,128]{1,0:T(8,128)}, f32[32,128]{1,0:T(8,128)}) custom-call(f32[32,32,512]{2,1,0:T(8,128)} %x_ref.1, f32[32,512]{1,0:T(8,128)} %ab_ref.1, f32[2,1024,512]{2,1,0:T(8,128)} %tiles_ref.1, s32[32]{0:T(128)} %bitcast.34, s32[32]{0:T(128)} %bitcast.35), custom_call_target="tpu_custom_call" | custom-call | tf_op jit(solution)/shard_map/pallas_call | solution.py:342
  44.4 0.8 %slice_bitcast_fusion.3 = (f32[32]{0:T(128)S(1)}, f32[32]{0:T(128)S(1)}, f32[32]{0:T(128)S(1)}) fusion(f32[8,128]{1,0:T(8,128)} %get-tuple-element.6), kind=kLoop, calls=%fused_computation.13 | loop fusion | bytes 768 | tf_op jit(solution)/shard_map/mul | solution.py:379
  45.2 0.0 copy-done
  45.2 0.0 copy-start.1
  45.3 6.5 %fusion.1 = (f32[32,32,512]{2,1,0:T(8,128)}, f32[32,32,512]{2,1,0:T(8,128)}) fusion(f32[32,32,512]{2,1,0:T(8,128)S(1)} %copy-done, f32[3,32,32,512]{3,2,1,0:T(8,128)} %get-tuple-element.7, f32[32]{0:T(128)S(1)} %get-tuple-element.15, f32[32]{0:T(128)S(1)} %get-tuple-element.16, f32[32]{0:T(128)S(1)} %get-tuple-element.14), kind=kLoop, calls=%fused_computation.2 | loop fusion | flops 5767168 | bytes 12583296 | tf_op jit(solution)/shard_map/sub | solution.py:380
  51.7 0.0 copy-done.1
  51.7 0.7 %copy.8 = f32[32,32]{1,0:T(8,128)} copy(f32[32,32]{0,1:T(8,128)S(1)} %slice_bitcast_fusion) | data formatting | bytes 8192
  (1 shorter events, 0.0 us)
Async XLA Ops:
  0.6 44.6 %copy-start = (f32[32,32,512]{2,1,0:T(8,128)S(1)}, f32[32,32,512]{2,1,0:T(8,128)}, u32[]{:S(2)}) copy-start(f32[32,32,512]{2,1,0:T(8,128)} %x_ref.1) | copy-start | bytes 6291460
  45.2 6.5 %copy-start.1 = (f32[32,128]{1,0:T(8,128)S(1)}, f32[32,128]{1,0:T(8,128)}, u32[]{:S(2)}) copy-start(f32[32,128]{1,0:T(8,128)} %get-tuple-element.8) | copy-start | bytes 49156

commit v3 on v2

--- a/solution.py
+++ b/solution.py
@@ -12,6 +12,7 @@
 RIDGE = 1e-05
 HALO = 3
 UNROLL = 14
+PIECES = 4
 
 
 def kernel(
@@ -253,8 +254,6 @@
             sk[j, g] = out[j * width:(j + 1) * width, :]
         return c
 
-    lax.fori_loop(0, ngx, mm, 0)
-
     def exchange(n, axis, pick, land, ss, rs):
         me = gx if axis == 0 else gy
         out = []
@@ -267,17 +266,47 @@
             c.start()
         return out
 
-    c1 = exchange(ngy, 1, lambda p: sk.at[p], part1, s1s, s1r)
-    total = sk[gy]
-    for k, c in enumerate(c1):
-        c.wait_recv()
-        total = total + part1[k]
-    mid[...] = total
-    c2 = exchange(ngx, 0, lambda p: mid.at[p], part2, s2s, s2r)
-    own = mid[gx]
-    for k, c in enumerate(c2):
-        c.wait_recv()
-        own = own + part2[k]
+    pieces = min(PIECES, ngx)
+    span = ngx // pieces
+    c1 = []
+    for b in range(pieces):
+        lax.fori_loop(b * span, (b + 1) * span, mm, 0)
+        part = slice(b * span, (b + 1) * span)
+        sends = []
+        for k in range(1, ngy):
+            peer = lax.rem(gy + k, ngy)
+            sends.append(pltpu.make_async_remote_copy(
+                src_ref=sk.at[peer, part], dst_ref=part1.at[k - 1, part],
+                send_sem=s1s.at[k - 1, b], recv_sem=s1r.at[k - 1, b],
+                device_id=(gx, peer), device_id_type=MESH))
+        for c in sends:
+            c.start()
+        c1.append(sends)
+
+    def to_owner(p, land):
+        return pltpu.make_async_remote_copy(
+            src_ref=mid.at[p], dst_ref=part2.at[land], send_sem=s2s.at[p], recv_sem=s2r.at[land],
+            device_id=(p, gy), device_id_type=MESH)
+
+    for b in range(pieces):
+        part = slice(b * span, (b + 1) * span)
+        total = sk[gy, part]
+        for k, c in enumerate(c1[b]):
+            c.wait_recv()
+            total = total + part1[k, part]
+        mid[part] = total
+        for p in range(b * span, (b + 1) * span):
+            @pl.when(p != gx)
+            def _(p=p):
+                to_owner(p, gx).start()
+    part2[gx] = mid[gx]
+    for p in range(ngx):
+        @pl.when(p != gx)
+        def _(p=p):
+            to_owner(p, p).wait_recv()
+    own = part2[0]
+    for p in range(1, ngx):
+        own = own + part2[p]
 
     prods = [jnp.sum(own * own, 0, keepdims=True)]
     for k in (1, 2):
@@ -316,7 +345,8 @@
     y1 = (f1 - l21 * y2) / p1
     y0 = (f0 - l10 * y1 - l20 * y2) / p0
 
-    skr_ref[...] = own - (y0 * pltpu.roll(own, 96, 1) + y1 * pltpu.roll(own, 64, 1) + y2 * pltpu.roll(own, 32, 1))
+    rest = own - (y0 * pltpu.roll(own, 96, 1) + y1 * pltpu.roll(own, 64, 1) + y2 * pltpu.roll(own, 32, 1))
+    skr_ref[...] = rest.T[0:32, :]
 
     y_ref[...] = jnp.concatenate([y0, y1, y2, jnp.zeros((5, 128), jnp.float32)], 0)
 
@@ -324,8 +354,12 @@
         @pl.when(to)
         def _(copy=copy):
             copy.wait_send()
-    for c in c1 + c2 + c3 + c4:
+    for c in sum(c1, []) + c3 + c4:
         c.wait_send()
+    for p in range(ngx):
+        @pl.when(p != gx)
+        def _(p=p):
+            to_owner(p, p).wait_send()
     for oc in out_copies:
         oc.wait()
 
@@ -344,7 +378,7 @@
         out_shape=(
             jax.ShapeDtypeStruct((3, count, rows, cols), f32),
             jax.ShapeDtypeStruct((8, 128), f32),
-            jax.ShapeDtypeStruct((width, 128), f32),
+            jax.ShapeDtypeStruct((count, width), f32),
         ),
         in_specs=[any_spec, vmem_spec, any_spec] + [pl.BlockSpec(memory_space=pltpu.SMEM)] * 2,
         out_specs=(any_spec, vmem_spec, vmem_spec),
@@ -362,13 +396,13 @@
             pltpu.VMEM((ngy, ngx, width, 128), f32),
             pltpu.VMEM((ngy - 1, ngx, width, 128), f32),
             pltpu.VMEM((ngx, width, 128), f32),
-            pltpu.VMEM((ngx - 1, width, 128), f32),
+            pltpu.VMEM((ngx, width, 128), f32),
             pltpu.VMEM((2, 8, 128), f32),
             pltpu.VMEM((ngy - 1, 8, 128), f32),
             pltpu.VMEM((ngx - 1, 8, 128), f32),
             pltpu.SMEM((2, ext), f32),
             dma((2,)), dma((3,)), dma((2,)), dma((2,)), dma((6,)), dma((6,)), dma((2,)), dma((2,)),
-            dma((ngy - 1,)), dma((ngy - 1,)), dma((ngx - 1,)), dma((ngx - 1,)),
+            dma((ngy - 1, PIECES)), dma((ngy - 1, PIECES)), dma((ngx,)), dma((ngx,)),
             dma((ngy - 1,)), dma((ngy - 1,)), dma((ngx - 1,)), dma((ngx - 1,)),
         ],
         compiler_params=pltpu.CompilerParams(
@@ -378,7 +412,7 @@
     c0, c1, c2 = [y[k, :count, None, None] for k in range(3)]
     solved = c0 * right_side + c1 * basis[0] + c2 * basis[1]
     left_over = right_side - (c0 * basis[0] + c1 * basis[1] + c2 * basis[2])
-    return solved, left_over, skr[:, :count].T
+    return solved, left_over, skr
 
 
 def solution(mesh):

time: 52.6 us -> 51.5 us (0.979)
  Pallas kernels: 43.8 us -> 42.8 us
    pallas_call x1, Pallas kernels: 43.8 us -> 42.8 us  [shards(): pl.pallas_call(functools.partial(kernel, ngx, ngy, rows, cols, width), ou...]
where the time goes in v3:
time: 51.5 us; the launch traced here: 51.3 us
  Pallas kernels  42.8 us (83%)
  other arithmetic  6.47 us (13%)
  local copies, waits for them, and re-layouts  1.41 us (3%)
  between operations  0.65 us (1%)
    pallas_call x1, Pallas kernels, shards(): pl.pallas_call(functools.partial(kernel, ngx, ngy, rows, cols, width), ou...  42.8 us
    sub x1, other arithmetic, shards(): left_over = right_side - (c0 * basis[0] + c1 * basis[1] + c2 * basis[2])  6.47 us

profile of v3, /device:TPU:0, one launch (start us, length us, event | category | flops | bytes accessed | tf_op | source)
XLA Modules:
  0.0 51.3 jit_solution(5480083896594854645)
XLA Ops:
  0.6 0.0 copy-start
  0.6 42.8 %shard_map.76 = (f32[3,32,32,512]{3,2,1,0:T(8,128)}, f32[8,128]{1,0:T(8,128)}, f32[32,32]{1,0:T(8,128)}) custom-call(f32[32,32,512]{2,1,0:T(8,128)} %x_ref.1, f32[32,512]{1,0:T(8,128)} %ab_ref.1, f32[2,1024,512]{2,1,0:T(8,128)} %tiles_ref.1, s32[32]{0:T(128)} %bitcast.32, s32[32]{0:T(128)} %bitcast.33), custom_call_target="tpu_custom_call" | custom-call | tf_op jit(solution)/shard_map/pallas_call | solution.py:376
  43.4 0.8 %slice_bitcast_fusion.2 = (f32[32]{0:T(128)S(1)}, f32[32]{0:T(128)S(1)}, f32[32]{0:T(128)S(1)}) fusion(f32[8,128]{1,0:T(8,128)} %get-tuple-element.6), kind=kLoop, calls=%fused_computation.12 | loop fusion | bytes 768 | tf_op jit(solution)/shard_map/mul | solution.py:413
  44.2 0.0 copy-done
  44.2 0.0 copy-start.1
  44.2 6.5 %fusion.1 = (f32[32,32,512]{2,1,0:T(8,128)}, f32[32,32,512]{2,1,0:T(8,128)}) fusion(f32[32,32,512]{2,1,0:T(8,128)S(1)} %copy-done, f32[3,32,32,512]{3,2,1,0:T(8,128)} %get-tuple-element.7, f32[32]{0:T(128)S(1)} %get-tuple-element.12, f32[32]{0:T(128)S(1)} %get-tuple-element.13, f32[32]{0:T(128)S(1)} %get-tuple-element.11), kind=kLoop, calls=%fused_computation.2 | loop fusion | flops 5767168 | bytes 12583296 | tf_op jit(solution)/shard_map/sub | solution.py:414
  50.7 0.0 copy-done.1
  50.7 0.6 %copy.9 = f32[32,32]{1,0:T(8,128)} copy(f32[32,32]{1,0:T(8,128)S(1)} %copy-done.1) | data formatting | bytes 8192
Async XLA Ops:
  0.6 43.6 %copy-start = (f32[32,32,512]{2,1,0:T(8,128)S(1)}, f32[32,32,512]{2,1,0:T(8,128)}, u32[]{:S(2)}) copy-start(f32[32,32,512]{2,1,0:T(8,128)} %x_ref.1) | copy-start | bytes 6291460
  44.2 6.5 %copy-start.1 = (f32[32,32]{1,0:T(8,128)S(1)}, f32[32,32]{1,0:T(8,128)}, u32[]{:S(2)}) copy-start(f32[32,32]{1,0:T(8,128)} %get-tuple-element.19) | copy-start | bytes 12292
